TPU v7x, 256 devices: a whole 4x4x8 slice. The times are simulated.
256 devices in a mesh: frame: 16 (over y, z_hi, core), row: 16 (over x, z_lo).
Axes of the slice: x: 4, y: 4, z: 8 (z_hi: 2, z_lo: 4; z = z_hi * 4 + z_lo), core: 2. Of those that a mesh axis runs over, the one named last changes fastest.
Arguments:
- spatial_q: bfloat16 [32, 128, 32, 1152], P('frame', 'row'), may hold values from -10.5 to 10.5
- spatial_k: bfloat16 [32, 128, 32, 1152], P('frame', 'row'), may hold values from -10.5 to 10.5
- spatial_v: bfloat16 [32, 128, 32, 1152], P('frame', 'row'), may hold values from -6 to 6
- residual: bfloat16 [32, 128, 32, 1152], P('frame', 'row'), may hold values from -6 to 6
- neighbour_list: int32 [64, 6], P('row'), may hold values from 0 to 15, as said below
- block_mask: int32 [8, 8], replicated, may hold values from 0 to 1, as said below
- out_weight: bfloat16 [1152, 1152], P('frame'), may hold values from -0.1875 to 0.1875
- qkv_weight: bfloat16 [1152, 3456], P('frame'), may hold values from -1.4799 to 1.4799
- pos_embed: float32 [32, 1152], P('frame'), may hold values from -150.5 to 150.5
- mod_shift: float32 [1152], replicated, may hold values from -2 to 2
- mod_scale: float32 [1152], replicated, may hold values from -2 to 2
Outputs:
- temporal_mix: bfloat16 [32, 128, 32, 1152], P('frame', 'row')
Inputs may be any that keep to these rules, and one draw needn't show every extreme that they name: `neighbour_list`: each row holds 6 different tiles of its own clip: slot 0 is the row's own tile; every other lies at most one tile row and at most two tile columns away from it, inside the grid of 16 tiles. `block_mask`: entry (i, j) is 1 where i == j and 0 where j > i.
All inputs are finite; a program needn't handle non-finite values.
Results may differ from a plain program's by a relative error of at most 0.0056.
The roundings to bfloat16 on the way count: a program that leaves them out, or rounds other values in their place, can miss the bound.
Values may be sent and summed in bfloat16 or wider, within the bound.
No kernel may reach another device: no remote copies, remote signals or barrier semaphores. Data moves between devices by JAX's collectives and lax.ppermute only.
A program may use at most 128 MiB of HBM per device.

v0:
```python
import math
import jax
import jax.numpy as jnp
from jax import lax
from jax.sharding import PartitionSpec as P

HEADS = 16
TILE = 8
SLOTS = 6
ROWS = 32
BLOCK = 4
EPS = 1e-06
ROW_AXIS = ("x", "zl")
FRAME_AXIS = ("y", "zh", "core")


def padded(block):
    count = lax.axis_size(ROW_AXIS)
    down = [(i, (i + 1) % count) for i in range(count) if (i + 1) % 4 != 3]
    up = [(target, source) for source, target in down]
    low = lax.ppermute(block, ROW_AXIS, down)
    high = lax.ppermute(block, ROW_AXIS, up)
    return jnp.concatenate([low, block, high], axis=2)


def gathered(weight):
    other = lax.ppermute(weight, ("zh", "zl"), [(i, 7 - i) for i in range(8)])
    first = lax.axis_index("zh") == 0
    pair = jnp.stack((jnp.where(first, weight, other), jnp.where(first, other, weight)), 0)
    full = lax.all_gather(pair, ("y", "core"), axis=0, tiled=False)
    rows, cols = weight.shape
    full = full.reshape(4, 2, 2, rows, cols)
    return jnp.transpose(full, (0, 2, 1, 3, 4)).reshape(16 * rows, cols)


def tiles_of(field):
    leading = field.shape[:-3]
    height, breadth, channels = field.shape[-3:]
    tile_grid = field.reshape(leading + (height // TILE, TILE, breadth // TILE, TILE, channels))
    lead_count = len(leading)
    arrangement = tuple(range(lead_count)) + (
        lead_count,
        lead_count + 2,
        lead_count + 1,
        lead_count + 3,
        lead_count + 4,
    )
    tile_grid = jnp.transpose(tile_grid, arrangement)
    return tile_grid.reshape(leading + (height // TILE * (breadth // TILE), TILE * TILE, channels))


def untile(tiles, height, breadth):
    leading = tiles.shape[:-3]
    channels = tiles.shape[-1]
    tile_grid = tiles.reshape(leading + (height // TILE, breadth // TILE, TILE, TILE, channels))
    lead_count = len(leading)
    arrangement = tuple(range(lead_count)) + (
        lead_count,
        lead_count + 2,
        lead_count + 1,
        lead_count + 3,
        lead_count + 4,
    )
    return jnp.transpose(tile_grid, arrangement).reshape(leading + (height, breadth, channels))


def window_attention(queries, keys, values):
    tile_count, token_count, channels = queries.shape
    head_size = channels // HEADS
    shaped_q = queries.reshape(tile_count, token_count, HEADS, head_size)
    shaped_k = keys.reshape(tile_count, -1, HEADS, head_size)
    shaped_v = values.reshape(tile_count, -1, HEADS, head_size)
    scores = jnp.einsum(
        "tqhe,tkhe->thqk", shaped_q, shaped_k, preferred_element_type=jnp.float32
    ) * (1.0 / math.sqrt(head_size))
    peak = jnp.max(scores, axis=-1, keepdims=True)
    powers = jnp.exp(scores - peak)
    weights = (powers / jnp.sum(powers, axis=-1, keepdims=True)).astype(jnp.bfloat16)
    mixed = jnp.einsum("thqk,tkhe->tqhe", weights, shaped_v, preferred_element_type=jnp.float32)
    return mixed.astype(jnp.bfloat16).reshape(tile_count, token_count, channels)


def frame_attention(queries, keys, values, allowed):
    frame_count, spot_count, channels = queries.shape
    head_size = channels // HEADS
    shaped_q = queries.reshape(frame_count, spot_count, HEADS, head_size)
    shaped_k = keys.reshape(frame_count, spot_count, HEADS, head_size)
    shaped_v = values.reshape(frame_count, spot_count, HEADS, head_size)
    scores = jnp.einsum(
        "fphe,gphe->phfg", shaped_q, shaped_k, preferred_element_type=jnp.float32
    ) * (1.0 / math.sqrt(head_size))
    scores = jnp.where(allowed, scores, -jnp.inf)
    peak = jnp.max(scores, axis=-1, keepdims=True)
    powers = jnp.exp(scores - peak)
    weights = (powers / jnp.sum(powers, axis=-1, keepdims=True)).astype(jnp.bfloat16)
    mixed = jnp.einsum("phfg,gphe->fphe", weights, shaped_v, preferred_element_type=jnp.float32)
    return mixed.astype(jnp.bfloat16).reshape(frame_count, spot_count, channels)


def normalize(field, mod_shift, mod_scale):
    average = jnp.mean(field, axis=-1, keepdims=True)
    centred = field - average
    spread = jnp.mean(centred * centred, axis=-1, keepdims=True)
    return centred * lax.rsqrt(spread + EPS) * (1.0 + mod_scale) + mod_shift


def fold_with(left, piece):
    return jnp.dot(left, piece, preferred_element_type=jnp.float32)


def frame_window(items):
    return window_attention(items[0], items[1], items[2])


def local(
    spatial_q,
    spatial_k,
    spatial_v,
    residual,
    neighbour_list,
    block_mask,
    out_weight,
    qkv_weight,
    pos_embed,
    mod_shift,
    mod_scale,
):
    frames_here, height, breadth, channels = spatial_q.shape
    tiles_wide = breadth // TILE
    tokens_here = frames_here * height * breadth
    stacked = jnp.stack((spatial_k, spatial_v), 0)
    rims = padded(stacked)
    key_tiles = tiles_of(rims)
    tile_row_here = (lax.axis_index(ROW_AXIS) + 1) % (ROWS // TILE)
    local_ids = (
        (neighbour_list // tiles_wide - tile_row_here + 1) * tiles_wide
        + neighbour_list % tiles_wide
    ).reshape(-1)
    picked = jnp.take(key_tiles, local_ids, axis=2).reshape(
        2, frames_here, tiles_wide, SLOTS * TILE * TILE, channels
    )
    query_tiles = tiles_of(spatial_q)
    attended = lax.map(frame_window, (query_tiles, picked[0], picked[1]))
    heads = untile(attended, height, breadth).reshape(tokens_here, channels)
    spatial_sum = fold_with(heads, gathered(out_weight))
    mixed = (residual.reshape(tokens_here, channels).astype(jnp.float32) + spatial_sum).astype(
        jnp.bfloat16
    )
    mixed = lax.optimization_barrier(mixed)
    shifted = (
        mixed.astype(jnp.float32).reshape(frames_here, height * breadth, channels)
        + pos_embed[:, None, :]
    )
    normed = normalize(shifted, mod_shift, mod_scale).astype(jnp.bfloat16)
    normed = lax.all_to_all(normed, FRAME_AXIS, split_axis=1, concat_axis=0, tiled=True)
    projected = fold_with(normed.reshape(tokens_here, channels), gathered(qkv_weight)).astype(
        jnp.bfloat16
    )
    projected = projected.reshape(-1, tokens_here // 32, 3 * channels)
    allowed = jnp.repeat(jnp.repeat(block_mask, BLOCK, axis=0), BLOCK, axis=1) == 1
    temporal = frame_attention(
        projected[..., :channels],
        projected[..., channels : 2 * channels],
        projected[..., 2 * channels :],
        allowed,
    )
    returned = lax.all_to_all(temporal, FRAME_AXIS, split_axis=0, concat_axis=1, tiled=True)
    return returned.reshape(frames_here, height, breadth, channels)


def solution(mesh):
    fine = jax.sharding.Mesh(mesh.devices.reshape(4, 2, 2, 4, 4), ("y", "zh", "core", "x", "zl"))
    tokens = P(FRAME_AXIS, ROW_AXIS, None, None)
    return jax.shard_map(
        local,
        mesh=fine,
        in_specs=(
            tokens,
            tokens,
            tokens,
            tokens,
            P(ROW_AXIS, None),
            P(),
            P(FRAME_AXIS, None),
            P(FRAME_AXIS, None),
            P(FRAME_AXIS, None),
            P(),
            P(),
        ),
        out_specs=tokens,
        check_vma=False,
    )
```

profile of v0, /device:TPU:39, one launch (start us, length us, event | category | flops | bytes accessed | tf_op | source)
XLA Modules:
  0.0 384.5 jit_solution(1866561831141859404)
XLA Ops:
  6.5 5.6 %collective-permute-start.2 = (bf16[72,1152]{1,0:T(8,128)(2,1)}, bf16[72,1152]{1,0:T(8,128)(2,1)S(1)}, u32[]{:S(2)}, u32[]{:S(2)}) collective-permute-start(bf16[72,1152]{1,0:T(8,128)(2,1)} %param.19), channel_id=1, source_target_pairs={{0,35},{1,34},{2,33},{3,32},{32,3},{33,2},{34,1},{35,0},{4,39},{5,... | collective-permute-start | bytes 497672 | tf_op jit(solution)/shard_map/ppermute | solution.py:27
  12.1 4.2 %collective-permute-done.2 = bf16[72,1152]{1,0:T(8,128)(2,1)S(1)} collective-permute-done((bf16[72,1152]{1,0:T(8,128)(2,1)}, bf16[72,1152]{1,0:T(8,128)(2,1)S(1)}, u32[]{:S(2)}, u32[]{:S(2)}) %collective-permute-start.2) | collective-permute-done | bytes 165920 | tf_op jit(solution)/shard_map/ppermute | solution.py:27
  23.6 5.0 %collective-permute-start.1 = (bf16[2,2,8,32,1152]{4,3,2,1,0:T(8,128)(2,1)}, bf16[2,2,8,32,1152]{4,3,2,1,0:T(8,128)(2,1)}, u32[]{:S(2)}, u32[]{:S(2)}) collective-permute-start(bf16[2,2,8,32,1152]{4,3,2,1,0:T(8,128)(2,1)} %pad_maximum_fusion.1), channel_id=1, source_target_pairs={{1,0},{2,1},{4,3},{5,4},{6,5},{8,7},{9,8},{10,9},{12,11},{13,12},{... | collective-permute-start | bytes 7077896 | tf_op jit(solution)/shard_map/ppermute | solution.py:22
  28.6 3.5 collective-permute-start.3
  34.1 106.8 %collective-permute-done.3 = bf16[72,3456]{1,0:T(8,128)(2,1)S(1)} collective-permute-done((bf16[72,3456]{1,0:T(8,128)(2,1)S(1)}, bf16[72,3456]{1,0:T(8,128)(2,1)S(1)}, u32[]{:S(2)}, u32[]{:S(2)}) %collective-permute-start.3) | collective-permute-done | bytes 497696 | tf_op jit(solution)/shard_map/ppermute | solution.py:27
  145.5 4.0 %copy.95 = bf16[2,2,3,4,8,8,1152]{6,5,4,3,2,1,0:T(8,128)(2,1)} copy(bf16[2,2,3,4,8,8,1152]{6,5,3,4,2,1,0:T(8,128)(2,1)S(1)} %bitcast.93) | data formatting | bytes 14155776 | tf_op jit(solution)/shard_map/transpose | solution.py:48
  149.5 10.5 %gather_fusion = bf16[24,2,2,64,1152]{4,3,2,1,0:T(8,128)(2,1)} fusion(bf16[2,2,12,64,1152]{4,3,2,1,0:T(8,128)(2,1)} %bitcast.92, s32[1024]{0:T(1024)S(1)} %pad_clamp_fusion), kind=kCustom, calls=%fused_computation | custom fusion | bytes 28311648 | tf_op jit(solution)/shard_map/jit(_take)/gather | solution.py:139
  160.0 7.1 %select_bitcast_fusion = bf16[2,2,24,64,1152]{4,3,1,0,2:T(8,128)(2,1)S(1)} fusion(bf16[24,2,2,64,1152]{4,3,2,1,0:T(8,128)(2,1)} %gather_fusion, pred[24]{0:T(512)(128)(4,1)S(1)} %compare_and_fusion), kind=kLoop, calls=%fused_computation.18 | loop fusion | flops 7077888 | bytes 28311576 | tf_op jit(solution)/shard_map/jit(_take)/select_n | solution.py:139
  168.6 3.6 copy.96
  172.2 3.6 copy.98
  175.8 73.6 %while.10 = (s32[]{:T(128)}, bf16[2,4,64,1152]{3,2,1,0:T(8,128)(2,1)}, bf16[2,4,384,1152]{3,2,1,0:T(8,128)(2,1)}, bf16[2,4,64,1152]{3,2,1,0:T(8,128)(2,1)}, bf16[2,4,384,1152]{3,2,1,0:T(8,128)(2,1)}, /*index=5*/s32[]{:T(128)}) while((s32[]{:T(128)}, bf16[2,4,64,1152]{3,2,1,0:T(8,128)(2,1)}, bf16[2,4,384,1152]{3,2,1,0:T(8,128)(2,1)}, ...), condition=%wide.region_3.4_spmd, body=%wide.region_0.3_spmd.sunk | while | flops 462717312 | bytes 77103232 | solution.py:143
  175.8 5.6 %constant_dynamic-slice_fusion.5 = (bf16[1,4,384,1152]{3,2,1,0:T(8,128)(2,1)}, bf16[1,4,384,1152]{3,2,1,0:T(8,128)(2,1)S(1)}) fusion(bf16[2,4,384,1152]{3,2,1,0:T(8,128)(2,1)} %get-tuple-element.138, s32[]{:T(128)} %get-tuple-element.128, bf16[2,4,384,1152]{3,2,1,0:T(8,128)(2,1)} %get-tuple-element.136), kind=kLoop, calls=%fused_computation.13.clone.1 | loop fusion | bytes 14155780 | tf_op jit(solution)/shard_map/while/body/jit(dynamic_index_in_dim)/dynamic_slice | solution.py:143
  181.5 5.8 %copy.134 = bf16[1,4,384,1152]{2,3,1,0:T(8,128)(2,1)} copy(bf16[1,4,384,1152]{3,2,1,0:T(8,128)(2,1)} %get-tuple-element.119) | data formatting | bytes 7077888 | tf_op jit(solution)/shard_map/while/body/jit(dynamic_index_in_dim)/dynamic_slice | solution.py:143
  189.2 3.7 reshape.191
  196.2 4.6 %fusion.56 = (f32[4,16,64]{2,1,0:T(8,128)}, f32[4,16,64,384]{3,2,1,0:T(8,128)}) fusion(f32[4,16,64,384]{3,2,1,0:T(8,128)S(1)} %fusion.55), kind=kOutput, calls=%fused_computation.72.clone.1 | output fusion | flops 6291839 | bytes 12599296 | tf_op jit(solution)/shard_map/while/body/eval_jaxpr/sub | solution.py:77
  200.8 3.6 copy.133
  204.4 5.3 %fusion.57 = bf16[4,64,16,72]{3,1,2,0:T(8,128)(2,1)S(1)} fusion(bf16[4,384,16,72]{1,3,2,0:T(8,128)(2,1)} %bitcast.89, f32[4,16,64,384]{3,2,1,0:T(8,128)} %get-tuple-element.120, f32[4,16,64]{2,1,0:T(8,128)} %get-tuple-element.121), kind=kOutput, calls=%fused_computation.9.clone.1 | convolution fusion | flops 229933056 | bytes 10436608 | tf_op jit(solution)/shard_map/while/body/eval_jaxpr/thqk,tkhe->tqhe/dot_general | solution.py:79
  212.7 5.5 %constant_dynamic-slice_fusion.5 = (bf16[1,4,384,1152]{3,2,1,0:T(8,128)(2,1)}, bf16[1,4,384,1152]{3,2,1,0:T(8,128)(2,1)S(1)}) fusion(bf16[2,4,384,1152]{3,2,1,0:T(8,128)(2,1)} %get-tuple-element.138, s32[]{:T(128)} %get-tuple-element.128, bf16[2,4,384,1152]{3,2,1,0:T(8,128)(2,1)} %get-tuple-element.136), kind=kLoop, calls=%fused_computation.13.clone.1 | loop fusion | bytes 14155780 | tf_op jit(solution)/shard_map/while/body/jit(dynamic_index_in_dim)/dynamic_slice | solution.py:143
  218.2 5.8 %copy.134 = bf16[1,4,384,1152]{2,3,1,0:T(8,128)(2,1)} copy(bf16[1,4,384,1152]{3,2,1,0:T(8,128)(2,1)} %get-tuple-element.119) | data formatting | bytes 7077888 | tf_op jit(solution)/shard_map/while/body/jit(dynamic_index_in_dim)/dynamic_slice | solution.py:143
  225.9 3.7 reshape.191
  232.9 4.6 %fusion.56 = (f32[4,16,64]{2,1,0:T(8,128)}, f32[4,16,64,384]{3,2,1,0:T(8,128)}) fusion(f32[4,16,64,384]{3,2,1,0:T(8,128)S(1)} %fusion.55), kind=kOutput, calls=%fused_computation.72.clone.1 | output fusion | flops 6291839 | bytes 12599296 | tf_op jit(solution)/shard_map/while/body/eval_jaxpr/sub | solution.py:77
  237.5 3.6 copy.133
  241.1 5.3 %fusion.57 = bf16[4,64,16,72]{3,1,2,0:T(8,128)(2,1)S(1)} fusion(bf16[4,384,16,72]{1,3,2,0:T(8,128)(2,1)} %bitcast.89, f32[4,16,64,384]{3,2,1,0:T(8,128)} %get-tuple-element.120, f32[4,16,64]{2,1,0:T(8,128)} %get-tuple-element.121), kind=kOutput, calls=%fused_computation.9.clone.1 | convolution fusion | flops 229933056 | bytes 10436608 | tf_op jit(solution)/shard_map/while/body/eval_jaxpr/thqk,tkhe->tqhe/dot_general | solution.py:79
  258.5 8.2 %all-to-all-start = ((bf16[2,256,1152]{2,0,1:T(2,128)(2,1)}), bf16[2,256,1152]{2,0,1:T(2,128)(2,1)S(1)}, u32[]{:S(2)}, u32[]{:S(2)}) async-start(bf16[2,256,1152]{2,0,1:T(2,128)(2,1)} %copy.103), calls=%async_computation | async-start | bytes 2359296 | tf_op jit(solution)/shard_map/all_to_all | solution.py:155
  266.8 33.2 %all-to-all-done = bf16[2,256,1152]{2,0,1:T(2,128)(2,1)S(1)} async-done(((bf16[2,256,1152]{2,0,1:T(2,128)(2,1)}), bf16[2,256,1152]{2,0,1:T(2,128)(2,1)S(1)}, u32[]{:S(2)}, u32[]{:S(2)}) %all-to-all-start) | async-done | bytes 1179680 | tf_op jit(solution)/shard_map/all_to_all | solution.py:155
  301.2 3.8 copy.106
  305.0 6.5 %convolution_convert_fusion = bf16[512,3456]{1,0:T(8,128)(2,1)S(1)} fusion(bf16[512,1152]{1,0:T(8,128)(2,1)} %bitcast.108, bf16[1152,3456]{1,0:T(8,128)(2,1)S(1)} %bitcast.96), kind=kOutput, calls=%fused_computation.20 | convolution fusion | flops 4078632960 | bytes 12681216 | tf_op jit(solution)/shard_map/dot_general | solution.py:108
  313.2 5.0 %reshape.173 = bf16[32,16,16,72]{3,2,1,0:T(8,128)(2,1)S(1)} reshape(bf16[32,16,1152]{2,1,0:T(8,128)(2,1)} %get-tuple-element.76) | data formatting | bytes 2359296 | tf_op jit(solution)/shard_map/reshape | solution.py:86
  318.2 5.7 %reshape.174 = bf16[32,16,16,72]{3,2,1,0:T(8,128)(2,1)} reshape(bf16[32,16,1152]{2,1,0:T(8,128)(2,1)} %get-tuple-element.75) | data formatting | bytes 2359296 | tf_op jit(solution)/shard_map/reshape | solution.py:87
  323.9 4.7 %reshape.172 = bf16[32,16,16,72]{3,2,1,0:T(8,128)(2,1)} reshape(bf16[32,16,1152]{2,1,0:T(8,128)(2,1)S(1)} %get-tuple-element.74) | data formatting | bytes 2359296 | tf_op jit(solution)/shard_map/reshape | solution.py:88
  328.6 4.3 %fusion.17 = f32[16,16,32,32]{2,3,1,0:T(8,128)S(1)} fusion(bf16[32,16,16,72]{3,2,1,0:T(8,128)(2,1)} %reshape.174, bf16[32,16,16,72]{3,2,1,0:T(8,128)(2,1)S(1)} %reshape.173), kind=kOutput, calls=%fused_computation.34 | convolution fusion | flops 37748736 | bytes 3407872 | tf_op jit(solution)/shard_map/fphe,gphe->phfg/dot_general | solution.py:89
  340.6 36.0 %all_to_all.30 = bf16[32,16,1152]{2,1,0:T(8,128)(2,1)S(1)} all-to-all(bf16[32,16,1152]{2,1,0:T(8,128)(2,1)} %reshape.175), channel_id=1, replica_groups=mesh['y'=4,'zh'=2,'core'=2,'x'=4,'zl'=4] {'y','zh','core'}, dimensions={0} | all-to-all | bytes 2359296 | tf_op jit(solution)/shard_map/all_to_all | solution.py:167
  (92 shorter events, 52.7 us)
Async XLA Ops:
  6.5 26.4 %copy-start = (bf16[2,8,32,1152]{3,2,1,0:T(8,128)(2,1)S(1)}, bf16[2,8,32,1152]{3,2,1,0:T(8,128)(2,1)}, u32[]{:S(2)}) copy-start(bf16[2,8,32,1152]{3,2,1,0:T(8,128)(2,1)} %param.13) | copy-start | bytes 3538948
  6.5 11.6 %copy-start.2 = (bf16[2,8,32,1152]{3,2,1,0:T(8,128)(2,1)S(1)}, bf16[2,8,32,1152]{3,2,1,0:T(8,128)(2,1)}, u32[]{:S(2)}) copy-start(bf16[2,8,32,1152]{3,2,1,0:T(8,128)(2,1)} %param.15) | copy-start | bytes 3538948
  6.5 244.3 %all-gather.5.cloned.1.call-start = ((), (), s32[]{:S(2)}) async-start(), calls=%async_computation.2 | async-start | bytes 2985984 | tf_op jit(solution)/shard_map/all_gather | solution.py:30
  6.5 9.8 %collective-permute-start.2 = (bf16[72,1152]{1,0:T(8,128)(2,1)}, bf16[72,1152]{1,0:T(8,128)(2,1)S(1)}, u32[]{:S(2)}, u32[]{:S(2)}) collective-permute-start(bf16[72,1152]{1,0:T(8,128)(2,1)} %param.19), channel_id=1, source_target_pairs={{0,35},{1,34},{2,33},{3,32},{32,3},{33,2},{34,1},{35,0},{4,39},{5,... | collective-permute-start | bytes 497672 | tf_op jit(solution)/shard_map/ppermute | solution.py:27
  18.1 283.1 %all-gather.7.cloned.1.call-start = ((), (), s32[]{:S(2)}) async-start(), calls=%async_computation.3 | async-start | bytes 8957952 | tf_op jit(solution)/shard_map/all_gather | solution.py:30
  18.1 10.5 %copy-start.7 = (bf16[72,3456]{1,0:T(8,128)(2,1)S(1)}, bf16[72,3456]{1,0:T(8,128)(2,1)}, u32[]{:S(2)}) copy-start(bf16[72,3456]{1,0:T(8,128)(2,1)} %param.20) | copy-start | bytes 1492996
  18.1 14.0 %copy-start.13 = (s32[4,6]{1,0:T(4,128)S(1)}, s32[4,6]{1,0:T(4,128)}, u32[]{:S(2)}) copy-start(s32[4,6]{1,0:T(4,128)} %param.17) | copy-start | bytes 292
  18.1 14.2 %copy-start.11 = (f32[1152]{0:T(1024)S(1)}, f32[1152]{0:T(1024)}, u32[]{:S(2)}) copy-start(f32[1152]{0:T(1024)} %param.23) | copy-start | bytes 13828
  21.1 120.9 %collective-permute-start = (bf16[2,2,8,32,1152]{4,3,2,1,0:T(8,128)(2,1)}, bf16[2,2,8,32,1152]{4,3,2,1,0:T(8,128)(2,1)}, u32[]{:S(2)}, u32[]{:S(2)}) collective-permute-start(bf16[2,2,8,32,1152]{4,3,2,1,0:T(8,128)(2,1)} %pad_maximum_fusion.1), channel_id=1, source_target_pairs={{0,1},{1,2},{3,4},{4,5},{5,6},{7,8},{8,9},{9,10},{11,12},{12,13},{... | collective-permute-start | bytes 7077896 | tf_op jit(solution)/shard_map/ppermute | solution.py:21
  23.6 118.4 %collective-permute-start.1 = (bf16[2,2,8,32,1152]{4,3,2,1,0:T(8,128)(2,1)}, bf16[2,2,8,32,1152]{4,3,2,1,0:T(8,128)(2,1)}, u32[]{:S(2)}, u32[]{:S(2)}) collective-permute-start(bf16[2,2,8,32,1152]{4,3,2,1,0:T(8,128)(2,1)} %pad_maximum_fusion.1), channel_id=1, source_target_pairs={{1,0},{2,1},{4,3},{5,4},{6,5},{8,7},{9,8},{10,9},{12,11},{13,12},{... | collective-permute-start | bytes 7077896 | tf_op jit(solution)/shard_map/ppermute | solution.py:22
  28.6 112.3 %collective-permute-start.3 = (bf16[72,3456]{1,0:T(8,128)(2,1)S(1)}, bf16[72,3456]{1,0:T(8,128)(2,1)S(1)}, u32[]{:S(2)}, u32[]{:S(2)}) collective-permute-start(bf16[72,3456]{1,0:T(8,128)(2,1)S(1)} %copy-done.7), channel_id=1, source_target_pairs={{0,35},{1,34},{2,33},{3,32},{32,3},{33,2},{34,1},{35,0},{4,39},{5,... | collective-permute-start | bytes 1493000 | tf_op jit(solution)/shard_map/ppermute | solution.py:27
  34.1 108.0 %copy-start.3 = (bf16[2,8,32,1152]{3,2,1,0:T(8,128)(2,1)S(1)}, bf16[2,8,32,1152]{3,2,1,0:T(8,128)(2,1)}, u32[]{:S(2)}) copy-start(bf16[2,8,32,1152]{3,2,1,0:T(8,128)(2,1)} %param.14) | copy-start | bytes 3538948
  209.7 2.0 copy-start.5
  211.7 1.0 copy-start.6
  246.4 2.0 copy-start.5
  248.4 1.0 copy-start.6
  250.9 2.1 copy-start.14
  253.0 1.9 copy-start.8
  254.8 0.9 copy-start.9
  254.8 0.9 copy-start.10
  256.2 10.4 %copy-start.12 = (s32[8,8]{1,0:T(8,128)S(1)}, s32[8,8]{1,0:T(8,128)}, u32[]{:S(2)}) copy-start(s32[8,8]{1,0:T(8,128)} %param.18) | copy-start | bytes 772
  258.5 41.5 %all-to-all-start = ((bf16[2,256,1152]{2,0,1:T(2,128)(2,1)}), bf16[2,256,1152]{2,0,1:T(2,128)(2,1)S(1)}, u32[]{:S(2)}, u32[]{:S(2)}) async-start(bf16[2,256,1152]{2,0,1:T(2,128)(2,1)} %copy.103), calls=%async_computation | async-start | bytes 2359296 | tf_op jit(solution)/shard_map/all_to_all | solution.py:155
  332.9 1.6 copy-start.4
  337.1 40.5 %copy-start.1 = (bf16[2,8,32,1152]{3,2,1,0:T(8,128)(2,1)S(1)}, bf16[2,8,32,1152]{3,2,1,0:T(8,128)(2,1)}, u32[]{:S(2)}) copy-start(bf16[2,8,32,1152]{3,2,1,0:T(8,128)(2,1)} %param.13) | copy-start | bytes 3538948
Sparse Core Ops, SparseCore 0:
  18.2 32.6 all-gather.4
  142.2 52.1 all-gather.6
where the time goes:
time: 386 us; the launch traced here: 385 us
  waiting for transfers between devices  144 us (37%)
  local copies, waits for them, and re-layouts  105 us (27%)
  blocking collectives  36 us (9%)
  matrix products  31.6 us (8%)
  other arithmetic  29 us (8%)
  starting transfers between devices  24.7 us (6%)
  between operations  13.7 us (4%)
    ppermute x2, waiting for transfers between devices, gathered(): other = lax.ppermute(weight, ('zh', 'zl'), [(i, 7 - i) for i in range(8)])  111 us
    all_to_all x1, blocking collectives, local(): lax.all_to_all(temporal, FRAME_AXIS, split_axis=0, concat_axis=1, tiled=T...  36 us
    dynamic_slice x8, local copies, waits for them, and re-layouts, local(): attended = lax.map(frame_window, (query_tiles, picked[0], picked[1]))  33.7 us
    all_to_all x1, waiting for transfers between devices, local(): lax.all_to_all(normed, FRAME_AXIS, split_axis=1, concat_axis=0, tiled=True)  33.2 us
    dot_general x2, matrix products, window_attention(): jnp.einsum('thqk,tkhe->tqhe', weights, shaped_v, preferred_element_type=j...  10.5 us
    gather x1, local copies, waits for them, and re-layouts, local(): jnp.take(key_tiles, local_ids, axis=2)  10.5 us
    sub x2, other arithmetic, window_attention(): powers = jnp.exp(scores - peak)  9.13 us
    ppermute x2, starting transfers between devices, gathered(): other = lax.ppermute(weight, ('zh', 'zl'), [(i, 7 - i) for i in range(8)])  9.05 us
  transfers between devices with their start and end apart: 7, of which 3 were waited for; matrix products, arithmetic and copies ran while one was open for 32% of the time, Pallas kernels for 0%

commit v1 on v0

--- a/solution.py
+++ b/solution.py
@@ -164,7 +164,10 @@
         projected[..., 2 * channels :],
         allowed,
     )
-    returned = lax.all_to_all(temporal, FRAME_AXIS, split_axis=0, concat_axis=1, tiled=True)
+    built = lax.all_to_all(
+        jnp.stack(jnp.split(temporal, lax.psum(1, FRAME_AXIS), 0), 0), FRAME_AXIS, 0, 0
+    )
+    returned = jnp.concatenate(built, 1)
     return returned.reshape(frames_here, height, breadth, channels)
 
 

time: 386 us -> 393 us (1.018); the launches traced: 385 us -> 387 us
  transfers between devices with their start and end apart: 7 -> 7, of which waited for: 3 -> 3; matrix products, arithmetic and copies ran while one was open for 32% -> 31% of each run, Pallas kernels for 0% -> 0%
where the time goes in v1:
time: 393 us; the launch traced here: 387 us
  waiting for transfers between devices  144 us (37%)
  local copies, waits for them, and re-layouts  107 us (27%)
  blocking collectives  35.9 us (9%)
  matrix products  31.6 us (8%)
  other arithmetic  29 us (7%)
  starting transfers between devices  24.6 us (6%)
  between operations  14.1 us (4%)
    ppermute x2, waiting for transfers between devices, gathered(): other = lax.ppermute(weight, ('zh', 'zl'), [(i, 7 - i) for i in range(8)])  111 us
    all_to_all x1, blocking collectives, local(): lax.all_to_all(jnp.stack(jnp.split(temporal, lax.psum(1, FRAME_AXIS), 0),...  35.9 us
    dynamic_slice x8, local copies, waits for them, and re-layouts, local(): attended = lax.map(frame_window, (query_tiles, picked[0], picked[1]))  33.8 us
    all_to_all x1, waiting for transfers between devices, local(): lax.all_to_all(normed, FRAME_AXIS, split_axis=1, concat_axis=0, tiled=True)  33.3 us
    dot_general x2, matrix products, window_attention(): jnp.einsum('thqk,tkhe->tqhe', weights, shaped_v, preferred_element_type=j...  10.5 us
    gather x1, local copies, waits for them, and re-layouts, local(): jnp.take(key_tiles, local_ids, axis=2)  10.5 us
    sub x2, other arithmetic, window_attention(): powers = jnp.exp(scores - peak)  9.15 us
    ppermute x2, starting transfers between devices, gathered(): other = lax.ppermute(weight, ('zh', 'zl'), [(i, 7 - i) for i in range(8)])  9.05 us
  transfers between devices with their start and end apart: 7, of which 3 were waited for; matrix products, arithmetic and copies ran while one was open for 31% of the time, Pallas kernels for 0%

profile of v1, /device:TPU:39, one launch (start us, length us, event | category | flops | bytes accessed | tf_op | source)
XLA Modules:
  0.0 387.0 jit_solution(1370045368260239863)
XLA Ops:
  6.5 5.6 %collective-permute-start.2 = (bf16[72,1152]{1,0:T(8,128)(2,1)}, bf16[72,1152]{1,0:T(8,128)(2,1)S(1)}, u32[]{:S(2)}, u32[]{:S(2)}) collective-permute-start(bf16[72,1152]{1,0:T(8,128)(2,1)} %param.19), channel_id=1, source_target_pairs={{0,35},{1,34},{2,33},{3,32},{32,3},{33,2},{34,1},{35,0},{4,39},{5,... | collective-permute-start | bytes 497672 | tf_op jit(solution)/shard_map/ppermute | solution.py:27
  12.1 4.2 %collective-permute-done.2 = bf16[72,1152]{1,0:T(8,128)(2,1)S(1)} collective-permute-done((bf16[72,1152]{1,0:T(8,128)(2,1)}, bf16[72,1152]{1,0:T(8,128)(2,1)S(1)}, u32[]{:S(2)}, u32[]{:S(2)}) %collective-permute-start.2) | collective-permute-done | bytes 165920 | tf_op jit(solution)/shard_map/ppermute | solution.py:27
  23.6 5.0 %collective-permute-start.1 = (bf16[2,2,8,32,1152]{4,3,2,1,0:T(8,128)(2,1)}, bf16[2,2,8,32,1152]{4,3,2,1,0:T(8,128)(2,1)}, u32[]{:S(2)}, u32[]{:S(2)}) collective-permute-start(bf16[2,2,8,32,1152]{4,3,2,1,0:T(8,128)(2,1)} %pad_maximum_fusion.1), channel_id=1, source_target_pairs={{1,0},{2,1},{4,3},{5,4},{6,5},{8,7},{9,8},{10,9},{12,11},{13,12},{... | collective-permute-start | bytes 7077896 | tf_op jit(solution)/shard_map/ppermute | solution.py:22
  28.6 3.5 collective-permute-start.3
  34.1 106.8 %collective-permute-done.3 = bf16[72,3456]{1,0:T(8,128)(2,1)S(1)} collective-permute-done((bf16[72,3456]{1,0:T(8,128)(2,1)S(1)}, bf16[72,3456]{1,0:T(8,128)(2,1)S(1)}, u32[]{:S(2)}, u32[]{:S(2)}) %collective-permute-start.3) | collective-permute-done | bytes 497696 | tf_op jit(solution)/shard_map/ppermute | solution.py:27
  145.5 4.0 %copy.155 = bf16[2,2,3,4,8,8,1152]{6,5,4,3,2,1,0:T(8,128)(2,1)} copy(bf16[2,2,3,4,8,8,1152]{6,5,3,4,2,1,0:T(8,128)(2,1)S(1)} %bitcast.121) | data formatting | bytes 14155776 | tf_op jit(solution)/shard_map/transpose | solution.py:48
  149.5 10.5 %gather_fusion = bf16[24,2,2,64,1152]{4,3,2,1,0:T(8,128)(2,1)} fusion(bf16[2,2,12,64,1152]{4,3,2,1,0:T(8,128)(2,1)} %bitcast.120, s32[1024]{0:T(1024)S(1)} %pad_clamp_fusion), kind=kCustom, calls=%fused_computation | custom fusion | bytes 28311648 | tf_op jit(solution)/shard_map/jit(_take)/gather | solution.py:139
  160.0 7.1 %select_bitcast_fusion = bf16[2,2,24,64,1152]{4,3,1,0,2:T(8,128)(2,1)S(1)} fusion(bf16[24,2,2,64,1152]{4,3,2,1,0:T(8,128)(2,1)} %gather_fusion, pred[24]{0:T(512)(128)(4,1)S(1)} %compare_and_fusion), kind=kLoop, calls=%fused_computation.18 | loop fusion | flops 7077888 | bytes 28311576 | tf_op jit(solution)/shard_map/jit(_take)/select_n | solution.py:139
  168.6 3.6 copy.156
  172.2 3.6 copy.158
  175.8 74.3 %while.10 = (s32[]{:T(128)}, bf16[2,4,64,1152]{3,2,1,0:T(8,128)(2,1)}, bf16[2,4,384,1152]{3,2,1,0:T(8,128)(2,1)}, bf16[2,4,64,1152]{3,2,1,0:T(8,128)(2,1)}, bf16[2,4,384,1152]{3,2,1,0:T(8,128)(2,1)}, /*index=5*/s32[]{:T(128)}) while((s32[]{:T(128)}, bf16[2,4,64,1152]{3,2,1,0:T(8,128)(2,1)}, bf16[2,4,384,1152]{3,2,1,0:T(8,128)(2,1)}, ...), condition=%wide.region_3.4_spmd, body=%wide.region_0.3_spmd.sunk | while | flops 462717312 | bytes 77103232 | solution.py:143
  176.3 5.6 %constant_dynamic-slice_fusion.5 = (bf16[1,4,384,1152]{3,2,1,0:T(8,128)(2,1)}, bf16[1,4,384,1152]{3,2,1,0:T(8,128)(2,1)S(1)}) fusion(bf16[2,4,384,1152]{3,2,1,0:T(8,128)(2,1)} %get-tuple-element.154, s32[]{:T(128)} %get-tuple-element.144, bf16[2,4,384,1152]{3,2,1,0:T(8,128)(2,1)} %get-tuple-element.152), kind=kLoop, calls=%fused_computation.13.clone.1 | loop fusion | bytes 14155780 | tf_op jit(solution)/shard_map/while/body/jit(dynamic_index_in_dim)/dynamic_slice | solution.py:143
  181.9 5.8 %copy.209 = bf16[1,4,384,1152]{2,3,1,0:T(8,128)(2,1)} copy(bf16[1,4,384,1152]{3,2,1,0:T(8,128)(2,1)} %get-tuple-element.135) | data formatting | bytes 7077888 | tf_op jit(solution)/shard_map/while/body/jit(dynamic_index_in_dim)/dynamic_slice | solution.py:143
  189.7 3.7 reshape.219
  196.7 4.6 %fusion.57 = (f32[4,16,64]{2,1,0:T(8,128)}, f32[4,16,64,384]{3,2,1,0:T(8,128)}) fusion(f32[4,16,64,384]{3,2,1,0:T(8,128)S(1)} %fusion.56), kind=kOutput, calls=%fused_computation.88.clone.1 | output fusion | flops 6291839 | bytes 12599296 | tf_op jit(solution)/shard_map/while/body/eval_jaxpr/sub | solution.py:77
  201.3 3.6 copy.208
  204.9 5.3 %fusion.58 = bf16[4,64,16,72]{3,1,2,0:T(8,128)(2,1)S(1)} fusion(bf16[4,384,16,72]{1,3,2,0:T(8,128)(2,1)} %bitcast.117, f32[4,16,64,384]{3,2,1,0:T(8,128)} %get-tuple-element.136, f32[4,16,64]{2,1,0:T(8,128)} %get-tuple-element.137), kind=kOutput, calls=%fused_computation.9.clone.1 | convolution fusion | flops 229933056 | bytes 10436608 | tf_op jit(solution)/shard_map/while/body/eval_jaxpr/thqk,tkhe->tqhe/dot_general | solution.py:79
  213.3 5.5 %constant_dynamic-slice_fusion.5 = (bf16[1,4,384,1152]{3,2,1,0:T(8,128)(2,1)}, bf16[1,4,384,1152]{3,2,1,0:T(8,128)(2,1)S(1)}) fusion(bf16[2,4,384,1152]{3,2,1,0:T(8,128)(2,1)} %get-tuple-element.154, s32[]{:T(128)} %get-tuple-element.144, bf16[2,4,384,1152]{3,2,1,0:T(8,128)(2,1)} %get-tuple-element.152), kind=kLoop, calls=%fused_computation.13.clone.1 | loop fusion | bytes 14155780 | tf_op jit(solution)/shard_map/while/body/jit(dynamic_index_in_dim)/dynamic_slice | solution.py:143
  218.8 5.8 %copy.209 = bf16[1,4,384,1152]{2,3,1,0:T(8,128)(2,1)} copy(bf16[1,4,384,1152]{3,2,1,0:T(8,128)(2,1)} %get-tuple-element.135) | data formatting | bytes 7077888 | tf_op jit(solution)/shard_map/while/body/jit(dynamic_index_in_dim)/dynamic_slice | solution.py:143
  226.5 3.7 reshape.219
  233.5 4.6 %fusion.57 = (f32[4,16,64]{2,1,0:T(8,128)}, f32[4,16,64,384]{3,2,1,0:T(8,128)}) fusion(f32[4,16,64,384]{3,2,1,0:T(8,128)S(1)} %fusion.56), kind=kOutput, calls=%fused_computation.88.clone.1 | output fusion | flops 6291839 | bytes 12599296 | tf_op jit(solution)/shard_map/while/body/eval_jaxpr/sub | solution.py:77
  238.1 3.6 copy.208
  241.7 5.3 %fusion.58 = bf16[4,64,16,72]{3,1,2,0:T(8,128)(2,1)S(1)} fusion(bf16[4,384,16,72]{1,3,2,0:T(8,128)(2,1)} %bitcast.117, f32[4,16,64,384]{3,2,1,0:T(8,128)} %get-tuple-element.136, f32[4,16,64]{2,1,0:T(8,128)} %get-tuple-element.137), kind=kOutput, calls=%fused_computation.9.clone.1 | convolution fusion | flops 229933056 | bytes 10436608 | tf_op jit(solution)/shard_map/while/body/eval_jaxpr/thqk,tkhe->tqhe/dot_general | solution.py:79
  259.2 8.1 %all-to-all-start = ((bf16[2,256,1152]{2,0,1:T(2,128)(2,1)}), bf16[2,256,1152]{2,0,1:T(2,128)(2,1)S(1)}, u32[]{:S(2)}, u32[]{:S(2)}) async-start(bf16[2,256,1152]{2,0,1:T(2,128)(2,1)} %copy.163), calls=%async_computation | async-start | bytes 2359296 | tf_op jit(solution)/shard_map/all_to_all | solution.py:155
  267.4 33.3 %all-to-all-done = bf16[2,256,1152]{2,0,1:T(2,128)(2,1)S(1)} async-done(((bf16[2,256,1152]{2,0,1:T(2,128)(2,1)}), bf16[2,256,1152]{2,0,1:T(2,128)(2,1)S(1)}, u32[]{:S(2)}, u32[]{:S(2)}) %all-to-all-start) | async-done | bytes 1179680 | tf_op jit(solution)/shard_map/all_to_all | solution.py:155
  301.9 3.8 copy.166
  305.7 6.5 %convolution_convert_fusion = bf16[512,3456]{1,0:T(8,128)(2,1)S(1)} fusion(bf16[512,1152]{1,0:T(8,128)(2,1)} %bitcast.136, bf16[1152,3456]{1,0:T(8,128)(2,1)S(1)} %bitcast.124), kind=kOutput, calls=%fused_computation.20 | convolution fusion | flops 4078632960 | bytes 12681216 | tf_op jit(solution)/shard_map/dot_general | solution.py:108
  313.9 5.0 %reshape.202 = bf16[32,16,16,72]{3,2,1,0:T(8,128)(2,1)S(1)} reshape(bf16[32,16,1152]{2,1,0:T(8,128)(2,1)} %get-tuple-element.76) | data formatting | bytes 2359296 | tf_op jit(solution)/shard_map/reshape | solution.py:86
  318.9 5.7 %reshape.203 = bf16[32,16,16,72]{3,2,1,0:T(8,128)(2,1)} reshape(bf16[32,16,1152]{2,1,0:T(8,128)(2,1)} %get-tuple-element.75) | data formatting | bytes 2359296 | tf_op jit(solution)/shard_map/reshape | solution.py:87
  324.6 4.9 %reshape.201 = bf16[32,16,16,72]{3,2,1,0:T(8,128)(2,1)} reshape(bf16[32,16,1152]{2,1,0:T(8,128)(2,1)S(1)} %get-tuple-element.74) | data formatting | bytes 2359296 | tf_op jit(solution)/shard_map/reshape | solution.py:88
  329.5 4.3 %fusion.17 = f32[16,16,32,32]{2,3,1,0:T(8,128)S(1)} fusion(bf16[32,16,16,72]{3,2,1,0:T(8,128)(2,1)} %reshape.203, bf16[32,16,16,72]{3,2,1,0:T(8,128)(2,1)S(1)} %reshape.202), kind=kOutput, calls=%fused_computation.34 | convolution fusion | flops 37748736 | bytes 3407872 | tf_op jit(solution)/shard_map/fphe,gphe->phfg/dot_general | solution.py:89
  342.9 35.9 %all_to_all.20 = bf16[16,2,16,1152]{3,2,1,0:T(8,128)(2,1)S(1)} all-to-all(bf16[16,2,16,1152]{3,2,1,0:T(8,128)(2,1)S(1)} %constant_dynamic-update-slice_fusion.1), channel_id=1, replica_groups=mesh['y'=4,'zh'=2,'core'=2,'x'=4,'zl'=4] {'y','zh','core'}, dimensions={0} | all-to-all | bytes 2359296 | tf_op jit(solution)/shard_map/all_to_all | solution.py:167
  (139 shorter events, 54.0 us)
Async XLA Ops:
  6.5 26.4 %copy-start = (bf16[2,8,32,1152]{3,2,1,0:T(8,128)(2,1)S(1)}, bf16[2,8,32,1152]{3,2,1,0:T(8,128)(2,1)}, u32[]{:S(2)}) copy-start(bf16[2,8,32,1152]{3,2,1,0:T(8,128)(2,1)} %param.13) | copy-start | bytes 3538948
  6.5 11.6 %copy-start.2 = (bf16[2,8,32,1152]{3,2,1,0:T(8,128)(2,1)S(1)}, bf16[2,8,32,1152]{3,2,1,0:T(8,128)(2,1)}, u32[]{:S(2)}) copy-start(bf16[2,8,32,1152]{3,2,1,0:T(8,128)(2,1)} %param.15) | copy-start | bytes 3538948
  6.5 245.1 %all-gather.5.cloned.1.call-start = ((), (), s32[]{:S(2)}) async-start(), calls=%async_computation.2 | async-start | bytes 2985984 | tf_op jit(solution)/shard_map/all_gather | solution.py:30
  6.5 9.8 %collective-permute-start.2 = (bf16[72,1152]{1,0:T(8,128)(2,1)}, bf16[72,1152]{1,0:T(8,128)(2,1)S(1)}, u32[]{:S(2)}, u32[]{:S(2)}) collective-permute-start(bf16[72,1152]{1,0:T(8,128)(2,1)} %param.19), channel_id=1, source_target_pairs={{0,35},{1,34},{2,33},{3,32},{32,3},{33,2},{34,1},{35,0},{4,39},{5,... | collective-permute-start | bytes 497672 | tf_op jit(solution)/shard_map/ppermute | solution.py:27
  18.1 283.9 %all-gather.7.cloned.1.call-start = ((), (), s32[]{:S(2)}) async-start(), calls=%async_computation.3 | async-start | bytes 8957952 | tf_op jit(solution)/shard_map/all_gather | solution.py:30
  18.1 10.5 %copy-start.7 = (bf16[72,3456]{1,0:T(8,128)(2,1)S(1)}, bf16[72,3456]{1,0:T(8,128)(2,1)}, u32[]{:S(2)}) copy-start(bf16[72,3456]{1,0:T(8,128)(2,1)} %param.20) | copy-start | bytes 1492996
  18.1 14.0 %copy-start.13 = (s32[4,6]{1,0:T(4,128)S(1)}, s32[4,6]{1,0:T(4,128)}, u32[]{:S(2)}) copy-start(s32[4,6]{1,0:T(4,128)} %param.17) | copy-start | bytes 292
  18.1 14.2 %copy-start.11 = (f32[1152]{0:T(1024)S(1)}, f32[1152]{0:T(1024)}, u32[]{:S(2)}) copy-start(f32[1152]{0:T(1024)} %param.23) | copy-start | bytes 13828
  21.1 121.0 %collective-permute-start = (bf16[2,2,8,32,1152]{4,3,2,1,0:T(8,128)(2,1)}, bf16[2,2,8,32,1152]{4,3,2,1,0:T(8,128)(2,1)}, u32[]{:S(2)}, u32[]{:S(2)}) collective-permute-start(bf16[2,2,8,32,1152]{4,3,2,1,0:T(8,128)(2,1)} %pad_maximum_fusion.1), channel_id=1, source_target_pairs={{0,1},{1,2},{3,4},{4,5},{5,6},{7,8},{8,9},{9,10},{11,12},{12,13},{... | collective-permute-start | bytes 7077896 | tf_op jit(solution)/shard_map/ppermute | solution.py:21
  23.6 118.4 %collective-permute-start.1 = (bf16[2,2,8,32,1152]{4,3,2,1,0:T(8,128)(2,1)}, bf16[2,2,8,32,1152]{4,3,2,1,0:T(8,128)(2,1)}, u32[]{:S(2)}, u32[]{:S(2)}) collective-permute-start(bf16[2,2,8,32,1152]{4,3,2,1,0:T(8,128)(2,1)} %pad_maximum_fusion.1), channel_id=1, source_target_pairs={{1,0},{2,1},{4,3},{5,4},{6,5},{8,7},{9,8},{10,9},{12,11},{13,12},{... | collective-permute-start | bytes 7077896 | tf_op jit(solution)/shard_map/ppermute | solution.py:22
  28.6 112.3 %collective-permute-start.3 = (bf16[72,3456]{1,0:T(8,128)(2,1)S(1)}, bf16[72,3456]{1,0:T(8,128)(2,1)S(1)}, u32[]{:S(2)}, u32[]{:S(2)}) collective-permute-start(bf16[72,3456]{1,0:T(8,128)(2,1)S(1)} %copy-done.7), channel_id=1, source_target_pairs={{0,35},{1,34},{2,33},{3,32},{32,3},{33,2},{34,1},{35,0},{4,39},{5,... | collective-permute-start | bytes 1493000 | tf_op jit(solution)/shard_map/ppermute | solution.py:27
  34.1 108.0 %copy-start.3 = (bf16[2,8,32,1152]{3,2,1,0:T(8,128)(2,1)S(1)}, bf16[2,8,32,1152]{3,2,1,0:T(8,128)(2,1)}, u32[]{:S(2)}) copy-start(bf16[2,8,32,1152]{3,2,1,0:T(8,128)(2,1)} %param.14) | copy-start | bytes 3538948
  210.2 2.0 copy-start.5
  212.3 1.0 copy-start.6
  247.0 2.0 copy-start.5
  249.0 1.0 copy-start.6
  251.6 2.1 copy-start.14
  253.7 1.9 copy-start.8
  255.5 0.9 copy-start.9
  255.6 0.9 copy-start.10
  257.0 10.3 %copy-start.12 = (s32[8,8]{1,0:T(8,128)S(1)}, s32[8,8]{1,0:T(8,128)}, u32[]{:S(2)}) copy-start(s32[8,8]{1,0:T(8,128)} %param.18) | copy-start | bytes 772
  259.2 41.5 %all-to-all-start = ((bf16[2,256,1152]{2,0,1:T(2,128)(2,1)}), bf16[2,256,1152]{2,0,1:T(2,128)(2,1)S(1)}, u32[]{:S(2)}, u32[]{:S(2)}) async-start(bf16[2,256,1152]{2,0,1:T(2,128)(2,1)} %copy.163), calls=%async_computation | async-start | bytes 2359296 | tf_op jit(solution)/shard_map/all_to_all | solution.py:155
  333.8 1.6 copy-start.4
  342.8 37.1 %copy-start.1 = (bf16[2,8,32,1152]{3,2,1,0:T(8,128)(2,1)S(1)}, bf16[2,8,32,1152]{3,2,1,0:T(8,128)(2,1)}, u32[]{:S(2)}) copy-start(bf16[2,8,32,1152]{3,2,1,0:T(8,128)(2,1)} %param.13) | copy-start | bytes 3538948
Sparse Core Ops, SparseCore 0:
  18.2 32.6 all-gather.4
  142.2 52.1 all-gather.6
